TPU v7x, 256 devices: a whole 4x4x8 slice. The times are simulated.
256 devices in a mesh: grp: 2 (over z_hi), mem: 128 (over x, z_lo, y, core).
Axes of the slice: x: 4, y: 4, z: 8 (z_hi: 2, z_lo: 4; z = z_hi * 4 + z_lo), core: 2. Of those that a mesh axis runs over, the one named last changes fastest.
Arguments:
- state_ens: bfloat16 [512, 131072], P('mem', 'grp'), may hold values from -6 to 6
- obs_ens: bfloat16 [512, 262144], P('mem', 'grp'), may hold values from -6 to 6
- obs_value: float32 [262144], P(('grp', 'mem')), may hold values from -12 to 12
- obs_class: int32 [262144], P(('grp', 'mem')), may hold values from 0 to 15
- loc_table: bfloat16 [16], replicated, may hold values from 0.049804688 to 1
- nbr_weight: float32 [4], replicated, may hold values from 0.25 to 1
Outputs:
- analysis: bfloat16 [512, 131072], P('mem', 'grp')
All inputs are finite; a program needn't handle non-finite values.
Results may differ from a plain program's by a relative error of at most 0.0065.
Values may be sent and summed in bfloat16 or wider, within the bound.
No kernel may reach another device: no remote copies, remote signals or barrier semaphores. Data moves between devices by JAX's collectives and lax.ppermute only.
A program may use at most 64 MiB of HBM per device.

v0:
```python
import jax
import jax.numpy as jnp
from jax import lax
from jax.experimental import pallas as pl
from jax.experimental.pallas import tpu as pltpu
from jax.sharding import PartitionSpec as P


MEMBERS = 512
CELLS = 512
LOCAL_OBS = 1024
ROW_PATCHES = 8
HALF = MEMBERS // 2
QUARTER = MEMBERS // 4
VEC = 16
PACKED = MEMBERS + VEC
F32 = jnp.float32
BF16 = jnp.bfloat16


def placement():
    order = []
    for row in range(16):
        z, step = row // 4, row % 4
        x = 3 - step if z % 2 == 0 else step
        order += [x * 32 + z * 8 + w for w in range(ROW_PATCHES)]
    return order


ORDER = placement()


def device_of(patch):
    return patch // 128 * 128 + ORDER[patch % 128]


def swaps(by, parity):
    pairs = []
    for p in range(256):
        row, column = p // ROW_PATCHES, p % ROW_PATCHES
        q = p + by
        if q < 256 and (by == ROW_PATCHES or q // ROW_PATCHES == row):
            if (row if by == ROW_PATCHES else column) % 2 == parity:
                pairs += [(device_of(p), device_of(q)), (device_of(q), device_of(p))]
    return pairs


def swap_weights(weight_ref):
    west, east, north, south = (weight_ref[k] for k in range(4))
    mem = lax.axis_index("mem")
    even_row = lax.rem(lax.div(mem, 32) + lax.div(mem, 8), 2) == 1
    even_column = lax.rem(mem, 2) == 0
    return (
        jnp.where(even_row, south, north),
        jnp.where(even_row, north, south),
        jnp.where(even_column, west, east),
        jnp.where(even_column, east, west),
    )


def lookup(classes, weight_table):
    codes = lax.broadcasted_iota(jnp.int32, (weight_table.shape[0], classes.shape[0]), 0)
    picked = jnp.where(codes == classes[None, :], weight_table.astype(F32)[:, None], 0.0)
    return jnp.sum(picked, axis=0)


def my_column():
    return lax.rem(lax.axis_index("mem"), ROW_PATCHES)


def split_kernel(state_ref, *rest):
    outs, sem = rest[:ROW_PATCHES], rest[ROW_PATCHES]
    copies = [
        pltpu.make_async_copy(state_ref.at[:, my_column() ^ d], outs[d], sem.at[d])
        for d in range(ROW_PATCHES)
    ]
    for copy in copies:
        copy.start()
    for copy in copies:
        copy.wait()


def merge_kernel(*refs):
    parts, out_ref, sem = refs[:ROW_PATCHES], refs[ROW_PATCHES], refs[ROW_PATCHES + 1]
    copies = [
        pltpu.make_async_copy(parts[d], out_ref.at[:, d], sem.at[d]) for d in range(ROW_PATCHES)
    ]
    for copy in copies:
        copy.start()
    for copy in copies:
        copy.wait()


def gather_rows(ref, rows_ref):
    width = rows_ref.shape[1]

    def step(i, acc):
        block = ref[pl.ds(i * 4, 4)].astype(F32)
        block = jnp.concatenate([block[:, 0], block[:, 1]], axis=1)
        rows_ref[pl.ds(pl.multiple_of(i * 32, 32), 32)] = block.reshape(32, width).astype(BF16)
        return acc + jnp.sum(block, axis=0)

    acc = lax.fori_loop(0, 16, step, jnp.zeros((8, width), F32))
    return jnp.sum(acc, axis=0, keepdims=True) / MEMBERS


def gram_kernel(obs_ref, val_ref, own_ref, send_ref, spread_ref, left_ref):
    centre = gather_rows(obs_ref, spread_ref)
    observed = val_ref[0:1]
    rates = val_ref[1:2]

    def step(i, carry):
        at = pl.ds(pl.multiple_of(i * 32, 32), 32)
        spread = (spread_ref[at].astype(F32) - centre).astype(BF16)
        spread_ref[at] = spread
        left_ref[at] = (spread.astype(F32) * rates).astype(BF16)
        return carry

    lax.fori_loop(0, 16, step, 0)
    innovation = (rates * (observed - centre)).astype(BF16)
    left_ref[pl.ds(MEMBERS, VEC)] = jnp.broadcast_to(innovation, (VEC, innovation.shape[1]))
    contract = (((1,), (1,)), ((), ()))
    first = lax.dot_general(
        left_ref[...], spread_ref[0:HALF], contract, preferred_element_type=F32
    )
    second = lax.dot_general(
        left_ref[HALF:], spread_ref[HALF:MEMBERS], contract, preferred_element_type=F32
    )
    row = lax.broadcasted_iota(jnp.int32, (QUARTER, QUARTER), 0)
    col = lax.broadcasted_iota(jnp.int32, (QUARTER, QUARTER), 1)

    def put(rows, columns, part):
        own_ref[rows, columns] = part
        send_ref[rows, columns] = part.astype(BF16)

    low, high = slice(0, QUARTER), slice(QUARTER, HALF)
    diagonals = []
    for part, columns in ((first, low), (second, high)):
        last = part[high, high]
        put(low, columns, jnp.where(row >= col, part[low, low], last.T))
        put(high, columns, part[high, low])
        diagonals.append(jnp.sum(jnp.where(row == col, last, 0.0), axis=0, keepdims=True))
    put(slice(HALF, MEMBERS), slice(0, HALF), first[HALF:MEMBERS])
    row = lax.broadcasted_iota(jnp.int32, (VEC, HALF), 0)
    tail = jnp.where(row < 8, first[MEMBERS:], second[HALF:])
    tail = jnp.where(row % 4 == 2, jnp.concatenate(diagonals, axis=1), tail)
    rounded = tail.astype(BF16).astype(F32)
    is_high = row % 8 < 4
    own_ref[MEMBERS:] = jnp.where(is_high, tail, 0.0)
    send_ref[MEMBERS:] = jnp.where(is_high, rounded, tail - rounded).astype(BF16)


def solve_kernel(
    weight_ref, own_ref, ns0_ref, ns1_ref, ew1_ref, ew0_ref, out_ref,
    sys_ref, t_ref, w_ref, w2_ref, tb_ref, wb_ref, w2b_ref, sb_ref, ub_ref,
):
    weights = swap_weights(weight_ref)

    def total(start, rows):
        at = pl.ds(start, rows)
        acc = own_ref[at]
        for k, ref in enumerate((ns0_ref, ns1_ref, ew1_ref, ew0_ref)):
            acc = acc + weights[k] * ref[at].astype(F32)
        return acc

    row = lax.broadcasted_iota(jnp.int32, (QUARTER, QUARTER), 0)
    col = lax.broadcasted_iota(jnp.int32, (QUARTER, QUARTER), 1)

    top, low, tail = total(0, QUARTER), total(QUARTER, QUARTER), total(MEMBERS, VEC)
    inflation = jnp.where(row == col, MEMBERS - 1.0, 0.0)
    diagonals = tail[2:3] + tail[6:7]
    for start, columns in ((0, slice(0, QUARTER)), (HALF, slice(QUARTER, HALF))):
        a, b, c = start, start + QUARTER, start + HALF
        square, cross = top[:, columns], low[:, columns]
        turned = square.T
        sys_ref[a:b, a:b] = jnp.where(row >= col, square, turned) + inflation
        square = jnp.where(row < col, square, turned)
        sys_ref[b:c, b:c] = jnp.where(row == col, diagonals[:, columns], square) + inflation
        sys_ref[b:c, a:b] = cross
        sys_ref[a:b, b:c] = cross.T
    cross = total(HALF, HALF)
    sys_ref[HALF:MEMBERS, 0:HALF] = cross
    sys_ref[0:HALF, HALF:MEMBERS] = cross.T
    rhs = jnp.concatenate([tail[0:1] + tail[4:5], tail[8:9] + tail[12:13]], axis=1)

    system = sys_ref[...]
    squares = jnp.sum(jnp.sum(system * system, axis=0, keepdims=True), axis=1, keepdims=True)
    norm = jnp.sqrt(squares)

    def dot(a, b):
        return jnp.dot(a[...], b[...], preferred_element_type=F32)

    def two_sweeps(w_ref, wb_ref):
        square = dot(tb_ref, tb_ref)
        sb_ref[...] = square.astype(BF16)
        ub_ref[...] = (0.0625 * square - 0.5625 * t_ref[...]).astype(BF16)
        w_ref[...] = 1.6875 * square - 2.4375 * t_ref[...]
        w = w_ref[...] + dot(ub_ref, sb_ref)
        w_ref[...] = w
        wb_ref[...] = w.astype(BF16)
        ub_ref[...] = (4.5 * w_ref[...] + dot(wb_ref, wb_ref)).astype(BF16)
        t = 5.0625 * t_ref[...] + dot(ub_ref, tb_ref)
        t_ref[...] = t
        tb_ref[...] = t.astype(BF16)

    t = system * (1.0 / norm)
    t_ref[...] = t
    tb_ref[...] = t.astype(BF16)
    two_sweeps(w_ref, wb_ref)
    two_sweeps(w2_ref, w2b_ref)
    w = 2.25 * (w_ref[...] + w2_ref[...]) + dot(wb_ref, w2b_ref)
    w_ref[...] = w
    wb_ref[...] = w.astype(BF16)
    w = 1.5 * w_ref[...] - 2.53125 * t_ref[...] - 0.5 * dot(wb_ref, tb_ref)

    row = lax.broadcasted_iota(jnp.int32, (MEMBERS, MEMBERS), 0)
    col = lax.broadcasted_iota(jnp.int32, (MEMBERS, MEMBERS), 1)
    root_inv = w + jnp.where(row == col, 1.5 * 5.0625, 0.0)
    half_step = jnp.sum(root_inv * rhs, axis=1, keepdims=True)
    mean_weight = jnp.sum(root_inv * half_step, axis=0, keepdims=True) / norm
    out_ref[...] = (jnp.sqrt((MEMBERS - 1.0) / norm) * root_inv + mean_weight).astype(BF16)


def update_kernel(transform_ref, state_ref, out_ref, dev_ref):
    column = my_column()

    def gather(i, acc):
        parts = [state_ref[i, column ^ w].astype(F32) for w in range(ROW_PATCHES)]
        block = jnp.concatenate(parts, axis=0)
        dev_ref[pl.ds(pl.multiple_of(i * 32, 32), 32)] = block.astype(BF16)
        return acc + jnp.sum(block.reshape(4, 8, CELLS), axis=0)

    acc = lax.fori_loop(0, 16, gather, jnp.zeros((8, CELLS), F32))
    centre = jnp.sum(acc, axis=0, keepdims=True) / MEMBERS
    dev_ref[...] = (dev_ref[...].astype(F32) - centre).astype(BF16)
    update = jnp.dot(transform_ref[...], dev_ref[...], preferred_element_type=F32)
    analysis = (centre + update).reshape(64, 8, CELLS)
    out_ref[:, 0] = analysis[:, 0:4].astype(BF16)
    out_ref[:, 1] = analysis[:, 4:8].astype(BF16)


def vmem(mebibytes):
    return pltpu.CompilerParams(vmem_limit_bytes=mebibytes * 2**20)


VMEM = pl.BlockSpec(memory_space=pltpu.VMEM)
HBM = pl.BlockSpec(memory_space=pltpu.HBM)
SMEM = pl.BlockSpec(memory_space=pltpu.SMEM)


def in_hbm(array):
    return pltpu.with_memory_space_constraint(array, pltpu.HBM)


def pallas(kernel, mebibytes, outs, in_specs, out_specs, scratch):
    return pl.pallas_call(
        kernel,
        out_shape=[jax.ShapeDtypeStruct(shape, dtype) for shape, dtype in outs],
        in_specs=in_specs,
        out_specs=out_specs,
        scratch_shapes=scratch,
        compiler_params=vmem(mebibytes),
    )


def shards(state_ens, obs_ens, obs_value, obs_class, loc_table, nbr_weight):
    obs = lax.all_to_all(
        obs_ens.reshape(4, 128, LOCAL_OBS), "mem", split_axis=1, concat_axis=0, tiled=False,
        axis_index_groups=[ORDER],
    ).reshape(64, 2, 4, LOCAL_OBS)
    values = jnp.stack([obs_value, lookup(obs_class, loc_table)])
    values = lax.ppermute(values, ("grp", "mem"), [(p, device_of(p)) for p in range(256)])

    part = (16, 4, CELLS)
    by_column = state_ens.reshape(4, 16, ROW_PATCHES, CELLS).transpose(1, 2, 0, 3)
    parts = list(pallas(
        split_kernel, 4, [(part, BF16)] * ROW_PATCHES, [HBM], [VMEM] * ROW_PATCHES,
        [pltpu.SemaphoreType.DMA((ROW_PATCHES,))],
    )(in_hbm(by_column)))
    for d in range(1, ROW_PATCHES):
        parts[d] = lax.ppermute(parts[d], "mem", [(k, k ^ d) for k in range(128)])
    (state,) = pallas(
        merge_kernel, 4, [((16, ROW_PATCHES, 4, CELLS), BF16)], [VMEM] * ROW_PATCHES, [HBM],
        [pltpu.SemaphoreType.DMA((ROW_PATCHES,))],
    )(*parts)
    state, obs, values = lax.optimization_barrier((state, obs, values))
    state = lax.all_to_all(
        state, "mem", split_axis=0, concat_axis=0, tiled=False,
        axis_index_groups=[ORDER[w::ROW_PATCHES] for w in range(ROW_PATCHES)],
    )

    packed = (PACKED, HALF)
    own, send = pallas(
        gram_kernel, 10, [(packed, F32), (packed, BF16)], [VMEM, VMEM], [VMEM, VMEM],
        [
            pltpu.VMEM((MEMBERS, LOCAL_OBS), BF16),
            pltpu.VMEM((MEMBERS + VEC, LOCAL_OBS), BF16),
        ],
    )(obs, values)
    received = []
    for (by, parity) in ((ROW_PATCHES, 0), (ROW_PATCHES, 1), (1, 1), (1, 0)):
        received.append(lax.ppermute(send, ("grp", "mem"), swaps(by, parity)))
    square = (MEMBERS, MEMBERS)
    (transform,) = pallas(
        solve_kernel, 16, [(square, BF16)], [SMEM] + [VMEM] * 5, [VMEM],
        [pltpu.VMEM(square, F32)] * 4 + [pltpu.VMEM(square, BF16)] * 5,
    )(nbr_weight, own, *received)
    (analysis,) = pallas(
        update_kernel, 8, [((64, 2, 4, CELLS), BF16)], [VMEM, VMEM], [VMEM],
        [pltpu.VMEM(square, BF16)],
    )(transform, state)
    back = lax.all_to_all(
        analysis.reshape(128, 4, CELLS), "mem", split_axis=0, concat_axis=1, tiled=False,
        axis_index_groups=[ORDER],
    )
    return back.reshape(4, 65536)


def solution(mesh):
    in_specs = (P("mem", "grp"), P("mem", "grp"), P(("grp", "mem")), P(("grp", "mem")), P(), P())
    out_specs = P("mem", "grp")
    return jax.shard_map(shards, mesh=mesh, in_specs=in_specs, out_specs=out_specs, check_vma=False)
```

profile of v0, /device:TPU:1, one launch (start us, length us, event | category | flops | bytes accessed | tf_op | source)
XLA Modules:
  0.0 97.3 jit_solution(16984011969274319760)
XLA Ops:
  0.0 14.6 %all-to-all-start = ((bf16[1,4,128,1024]{3,1,0,2:T(4,128)(2,1)}), bf16[1,4,128,1024]{3,1,0,2:T(4,128)(2,1)S(1)}, u32[]{:S(2)}, u32[]{:S(2)}) async-start(bf16[1,4,128,1024]{3,1,0,2:T(4,128)(2,1)} %bitcast.22), calls=%async_computation | async-start | bytes 2097152 | tf_op jit(solution)/shard_map/all_to_all | solution.py:267
  14.6 1.1 %shard_map.64 = (bf16[16,4,512]{2,1,0:T(4,128)(2,1)S(1)}, bf16[16,4,512]{2,1,0:T(4,128)(2,1)S(1)}, bf16[16,4,512]{2,1,0:T(4,128)(2,1)S(1)}, bf16[16,4,512]{2,1,0...) custom-call(bf16[16,8,4,512]{3,2,1,0:T(4,128)(2,1)} %bitcast.23), custom_call_target="tpu_custom_call" | custom-call | tf_op jit(solution)/shard_map/pallas_call | solution.py:276
  15.8 0.5 collective-permute-start
  16.3 0.0 copy-start.1
  16.3 1.2 %collective-permute-start.1 = (bf16[16,4,512]{2,1,0:T(4,128)(2,1)S(1)}, bf16[16,4,512]{2,1,0:T(4,128)(2,1)S(1)}, u32[]{:S(2)}, u32[]{:S(2)}) collective-permute-start(bf16[16,4,512]{2,1,0:T(4,128)(2,1)S(1)} %get-tuple-element.20), channel_id=1, source_target_pairs={{0,2},{1,3},{2,0},{3,1},{4,6},{5,7},{6,4},{7,5},{8,10},{9,11},{10,... | collective-permute-start | bytes 196616 | tf_op jit(solution)/shard_map/ppermute | solution.py:281
  17.5 0.6 collective-permute-start.2
  18.0 0.0 copy-start.3
  18.0 2.7 %collective-permute-start.3 = (bf16[16,4,512]{2,1,0:T(4,128)(2,1)S(1)}, bf16[16,4,512]{2,1,0:T(4,128)(2,1)S(1)}, u32[]{:S(2)}, u32[]{:S(2)}) collective-permute-start(bf16[16,4,512]{2,1,0:T(4,128)(2,1)S(1)} %get-tuple-element.22), channel_id=1, source_target_pairs={{0,4},{1,5},{2,6},{3,7},{4,0},{5,1},{6,2},{7,3},{8,12},{9,13},{10,... | collective-permute-start | bytes 196616 | tf_op jit(solution)/shard_map/ppermute | solution.py:281
  20.7 0.5 collective-permute-start.4
  21.3 0.0 copy-done.3
  21.3 0.0 copy-done.1
  21.3 0.1 select_reduce_fusion
  21.4 0.0 copy-start.2
  21.4 0.0 collective-permute-done.refs_1_
  21.4 2.5 %collective-permute-start.5 = (bf16[16,4,512]{2,1,0:T(4,128)(2,1)S(1)}, bf16[16,4,512]{2,1,0:T(4,128)(2,1)S(1)}, u32[]{:S(2)}, u32[]{:S(2)}) collective-permute-start(bf16[16,4,512]{2,1,0:T(4,128)(2,1)S(1)} %get-tuple-element.24), channel_id=1, source_target_pairs={{0,6},{1,7},{2,4},{3,5},{4,2},{5,3},{6,0},{7,1},{8,14},{9,15},{10,... | collective-permute-start | bytes 196616 | tf_op jit(solution)/shard_map/ppermute | solution.py:281
  23.9 0.0 collective-permute-done.1.refs_2_
  23.9 2.0 %collective-permute-start.6 = (bf16[16,4,512]{2,1,0:T(4,128)(2,1)S(1)}, bf16[16,4,512]{2,1,0:T(4,128)(2,1)S(1)}, u32[]{:S(2)}, u32[]{:S(2)}) collective-permute-start(bf16[16,4,512]{2,1,0:T(4,128)(2,1)S(1)} %get-tuple-element.25), channel_id=1, source_target_pairs={{0,7},{1,6},{2,5},{3,4},{4,3},{5,2},{6,1},{7,0},{8,15},{9,14},{10,... | collective-permute-start | bytes 196616 | tf_op jit(solution)/shard_map/ppermute | solution.py:281
  25.9 0.0 copy-done.2
  26.0 1.0 %collective-permute-done.2.refs_3_ = bf16[16,4,512]{2,1,0:T(4,128)(2,1)S(1)} collective-permute-done((bf16[16,4,512]{2,1,0:T(4,128)(2,1)S(1)}, bf16[16,4,512]{2,1,0:T(4,128)(2,1)S(1)}, u32[]{:S(2)}, u32[]{:S(2)}) %collective-permute-start.2) | collective-permute-done | bytes 65568 | tf_op jit(solution)/shard_map/ppermute | solution.py:281
  27.0 2.9 %collective-permute-start.7 = (f32[2,1024]{1,0:T(2,128)S(1)}, f32[2,1024]{1,0:T(2,128)S(1)}, u32[]{:S(2)}, u32[]{:S(2)}) collective-permute-start(f32[2,1024]{1,0:T(2,128)S(1)} %pad_maximum_fusion), channel_id=1, source_target_pairs={{0,96},{1,97},{2,98},{3,99},{4,100},{5,101},{6,102},{7,103},{8,64}... | collective-permute-start | bytes 24584 | tf_op jit(solution)/shard_map/ppermute | solution.py:272
  29.9 0.3 collective-permute-done.3.refs_4_
  30.2 2.0 %collective-permute-done.4.refs_5_ = bf16[16,4,512]{2,1,0:T(4,128)(2,1)S(1)} collective-permute-done((bf16[16,4,512]{2,1,0:T(4,128)(2,1)S(1)}, bf16[16,4,512]{2,1,0:T(4,128)(2,1)S(1)}, u32[]{:S(2)}, u32[]{:S(2)}) %collective-permute-start.4) | collective-permute-done | bytes 65568 | tf_op jit(solution)/shard_map/ppermute | solution.py:281
  32.2 0.0 collective-permute-done.5.refs_6_
  32.2 2.4 %collective-permute-done.6.refs_7_ = bf16[16,4,512]{2,1,0:T(4,128)(2,1)S(1)} collective-permute-done((bf16[16,4,512]{2,1,0:T(4,128)(2,1)S(1)}, bf16[16,4,512]{2,1,0:T(4,128)(2,1)S(1)}, u32[]{:S(2)}, u32[]{:S(2)}) %collective-permute-start.6) | collective-permute-done | bytes 65568 | tf_op jit(solution)/shard_map/ppermute | solution.py:281
  34.6 0.8 shard_map.65
  35.4 0.0 collective-permute-done.7.val_ref
  35.4 6.9 %all-to-all-done = bf16[1,4,128,1024]{3,1,0,2:T(4,128)(2,1)S(1)} async-done(((bf16[1,4,128,1024]{3,1,0,2:T(4,128)(2,1)}), bf16[1,4,128,1024]{3,1,0,2:T(4,128)(2,1)S(1)}, u32[]{:S(2)}, u32[]{:S(2)}) %all-to-all-start) | async-done | bytes 1048608 | tf_op jit(solution)/shard_map/all_to_all | solution.py:267
  42.4 5.3 %all-to-all-start.1 = ((bf16[16,8,4,512]{3,2,1,0:T(4,128)(2,1)}), bf16[16,8,4,512]{3,2,1,0:T(4,128)(2,1)S(1)}, u32[]{:S(2)}, u32[]{:S(2)}) async-start(bf16[16,8,4,512]{3,2,1,0:T(4,128)(2,1)} %shard_map.65), calls=%async_computation.1 | async-start | bytes 1048576 | tf_op jit(solution)/shard_map/all_to_all | solution.py:287
  47.7 1.5 %shard_map.66 = (f32[528,256]{1,0:T(8,128)S(1)}, bf16[528,256]{1,0:T(8,128)(2,1)S(1)}) custom-call(bf16[64,2,4,1024]{3,2,1,0:T(4,128)(2,1)S(1)} %bitcast.19, f32[2,1024]{1,0:T(2,128)S(1)} %collective-permute-done.7.val_ref), custom_call_target="tpu_custom_call" | custom-call | tf_op jit(solution)/shard_map/pallas_call | solution.py:293
  49.2 0.0 copy-start
  49.2 1.7 %collective-permute-start.11 = (bf16[528,256]{1,0:T(8,128)(2,1)S(1)}, bf16[528,256]{1,0:T(8,128)(2,1)S(1)}, u32[]{:S(2)}, u32[]{:S(2)}) collective-permute-start(bf16[528,256]{1,0:T(8,128)(2,1)S(1)} %get-tuple-element.29), channel_id=1, source_target_pairs={{96,97},{97,96},{98,99},{99,98},{100,101},{101,100},{102,103},{103... | collective-permute-start | bytes 811016 | tf_op jit(solution)/shard_map/ppermute | solution.py:302
  50.9 1.9 %collective-permute-start.10 = (bf16[528,256]{1,0:T(8,128)(2,1)S(1)}, bf16[528,256]{1,0:T(8,128)(2,1)S(1)}, u32[]{:S(2)}, u32[]{:S(2)}) collective-permute-start(bf16[528,256]{1,0:T(8,128)(2,1)S(1)} %get-tuple-element.29), channel_id=1, source_target_pairs={{97,98},{98,97},{99,100},{100,99},{101,102},{102,101},{65,66},{66,... | collective-permute-start | bytes 811016 | tf_op jit(solution)/shard_map/ppermute | solution.py:302
  52.8 3.1 %collective-permute-start.9 = (bf16[528,256]{1,0:T(8,128)(2,1)S(1)}, bf16[528,256]{1,0:T(8,128)(2,1)S(1)}, u32[]{:S(2)}, u32[]{:S(2)}) collective-permute-start(bf16[528,256]{1,0:T(8,128)(2,1)S(1)} %get-tuple-element.29), channel_id=1, source_target_pairs={{64,32},{32,64},{65,33},{33,65},{66,34},{34,66},{67,35},{35,67},{6... | collective-permute-start | bytes 811016 | tf_op jit(solution)/shard_map/ppermute | solution.py:302
  55.9 0.1 collective-permute-start.8
  56.0 0.0 collective-permute-done.11.ew0_ref
  56.0 2.9 %collective-permute-done.10.ew1_ref = bf16[528,256]{1,0:T(8,128)(2,1)S(1)} collective-permute-done((bf16[528,256]{1,0:T(8,128)(2,1)S(1)}, bf16[528,256]{1,0:T(8,128)(2,1)S(1)}, u32[]{:S(2)}, u32[]{:S(2)}) %collective-permute-start.10) | collective-permute-done | bytes 270368 | tf_op jit(solution)/shard_map/ppermute | solution.py:302
  59.0 5.9 %collective-permute-done.9.ns1_ref = bf16[528,256]{1,0:T(8,128)(2,1)S(1)} collective-permute-done((bf16[528,256]{1,0:T(8,128)(2,1)S(1)}, bf16[528,256]{1,0:T(8,128)(2,1)S(1)}, u32[]{:S(2)}, u32[]{:S(2)}) %collective-permute-start.9) | collective-permute-done | bytes 270368 | tf_op jit(solution)/shard_map/ppermute | solution.py:302
  64.9 0.0 collective-permute-done.8.ns0_ref
  64.9 0.0 copy-done
  64.9 4.8 %shard_map.67.transform_ref = bf16[512,512]{1,0:T(8,128)(2,1)S(1)} custom-call(f32[4]{0:T(128)S(1)} %copy-done, f32[528,256]{1,0:T(8,128)S(1)} %get-tuple-element.28.own_ref, bf16[528,256]{1,0:T(8,128)(2,1)S(1)} %collective-permute-done.8.ns0_ref, bf16[528,256]{1,0:T(8,128)(2,1)S(1)} %collective-permute-done.9.ns1_ref, ...), custom_call_target="tpu_custom_call" | custom-call | tf_op jit(solution)/shard_map/pallas_call | solution.py:304
  69.7 0.0 all-to-all-done.1.state_ref
  69.7 0.8 shard_map.68
  70.5 26.0 %all_to_all.35 = bf16[128,4,1,512]{3,1,2,0:T(4,128)(2,1)S(1)} all-to-all(bf16[128,4,1,512]{3,1,2,0:T(4,128)(2,1)S(1)} %bitcast.20), channel_id=1, replica_groups={{96,97,98,99,100,101,102,103,64,65,66,67,68,69,70,71,32,33,34,35,36,37,..., dimensions={0} | all-to-all | bytes 1048576 | tf_op jit(solution)/shard_map/all_to_all | solution.py:312
  96.5 0.8 copy.12
  (2 shorter events, 0.0 us)
Async XLA Ops:
  0.0 42.4 %all-to-all-start = ((bf16[1,4,128,1024]{3,1,0,2:T(4,128)(2,1)}), bf16[1,4,128,1024]{3,1,0,2:T(4,128)(2,1)S(1)}, u32[]{:S(2)}, u32[]{:S(2)}) async-start(bf16[1,4,128,1024]{3,1,0,2:T(4,128)(2,1)} %bitcast.22), calls=%async_computation | async-start | bytes 2097152 | tf_op jit(solution)/shard_map/all_to_all | solution.py:267
  15.8 5.6 %collective-permute-start = (bf16[16,4,512]{2,1,0:T(4,128)(2,1)S(1)}, bf16[16,4,512]{2,1,0:T(4,128)(2,1)S(1)}, u32[]{:S(2)}, u32[]{:S(2)}) collective-permute-start(bf16[16,4,512]{2,1,0:T(4,128)(2,1)S(1)} %get-tuple-element.19), channel_id=1, source_target_pairs={{0,1},{1,0},{2,3},{3,2},{4,5},{5,4},{6,7},{7,6},{8,9},{9,8},{10,11... | collective-permute-start | bytes 196616 | tf_op jit(solution)/shard_map/ppermute | solution.py:281
  16.3 5.0 %copy-start.1 = (s32[1024]{0:T(1024)S(1)}, s32[1024]{0:T(1024)}, u32[]{:S(2)}) copy-start(s32[1024]{0:T(1024)} %param.9) | copy-start | bytes 12292
  16.3 7.6 %collective-permute-start.1 = (bf16[16,4,512]{2,1,0:T(4,128)(2,1)S(1)}, bf16[16,4,512]{2,1,0:T(4,128)(2,1)S(1)}, u32[]{:S(2)}, u32[]{:S(2)}) collective-permute-start(bf16[16,4,512]{2,1,0:T(4,128)(2,1)S(1)} %get-tuple-element.20), channel_id=1, source_target_pairs={{0,2},{1,3},{2,0},{3,1},{4,6},{5,7},{6,4},{7,5},{8,10},{9,11},{10,... | collective-permute-start | bytes 196616 | tf_op jit(solution)/shard_map/ppermute | solution.py:281
  17.5 9.5 %collective-permute-start.2 = (bf16[16,4,512]{2,1,0:T(4,128)(2,1)S(1)}, bf16[16,4,512]{2,1,0:T(4,128)(2,1)S(1)}, u32[]{:S(2)}, u32[]{:S(2)}) collective-permute-start(bf16[16,4,512]{2,1,0:T(4,128)(2,1)S(1)} %get-tuple-element.21), channel_id=1, source_target_pairs={{0,3},{1,2},{2,1},{3,0},{4,7},{5,6},{6,5},{7,4},{8,11},{9,10},{10,... | collective-permute-start | bytes 196616 | tf_op jit(solution)/shard_map/ppermute | solution.py:281
  18.0 3.2 %copy-start.3 = (bf16[16]{0:T(256)(128)(2,1)S(1)}, bf16[16]{0:T(256)(128)(2,1)}, u32[]{:S(2)}) copy-start(bf16[16]{0:T(256)(128)(2,1)} %param.10) | copy-start | bytes 100
  18.0 12.1 %collective-permute-start.3 = (bf16[16,4,512]{2,1,0:T(4,128)(2,1)S(1)}, bf16[16,4,512]{2,1,0:T(4,128)(2,1)S(1)}, u32[]{:S(2)}, u32[]{:S(2)}) collective-permute-start(bf16[16,4,512]{2,1,0:T(4,128)(2,1)S(1)} %get-tuple-element.22), channel_id=1, source_target_pairs={{0,4},{1,5},{2,6},{3,7},{4,0},{5,1},{6,2},{7,3},{8,12},{9,13},{10,... | collective-permute-start | bytes 196616 | tf_op jit(solution)/shard_map/ppermute | solution.py:281
  20.7 11.4 %collective-permute-start.4 = (bf16[16,4,512]{2,1,0:T(4,128)(2,1)S(1)}, bf16[16,4,512]{2,1,0:T(4,128)(2,1)S(1)}, u32[]{:S(2)}, u32[]{:S(2)}) collective-permute-start(bf16[16,4,512]{2,1,0:T(4,128)(2,1)S(1)} %get-tuple-element.23), channel_id=1, source_target_pairs={{0,5},{1,4},{2,7},{3,6},{4,1},{5,0},{6,3},{7,2},{8,13},{9,12},{10,... | collective-permute-start | bytes 196616 | tf_op jit(solution)/shard_map/ppermute | solution.py:281
  21.4 4.6 %copy-start.2 = (f32[1024]{0:T(1024)S(1)}, f32[1024]{0:T(1024)}, u32[]{:S(2)}) copy-start(f32[1024]{0:T(1024)} %param.8) | copy-start | bytes 12292
  21.4 10.8 %collective-permute-start.5 = (bf16[16,4,512]{2,1,0:T(4,128)(2,1)S(1)}, bf16[16,4,512]{2,1,0:T(4,128)(2,1)S(1)}, u32[]{:S(2)}, u32[]{:S(2)}) collective-permute-start(bf16[16,4,512]{2,1,0:T(4,128)(2,1)S(1)} %get-tuple-element.24), channel_id=1, source_target_pairs={{0,6},{1,7},{2,4},{3,5},{4,2},{5,3},{6,0},{7,1},{8,14},{9,15},{10,... | collective-permute-start | bytes 196616 | tf_op jit(solution)/shard_map/ppermute | solution.py:281
  23.9 10.7 %collective-permute-start.6 = (bf16[16,4,512]{2,1,0:T(4,128)(2,1)S(1)}, bf16[16,4,512]{2,1,0:T(4,128)(2,1)S(1)}, u32[]{:S(2)}, u32[]{:S(2)}) collective-permute-start(bf16[16,4,512]{2,1,0:T(4,128)(2,1)S(1)} %get-tuple-element.25), channel_id=1, source_target_pairs={{0,7},{1,6},{2,5},{3,4},{4,3},{5,2},{6,1},{7,0},{8,15},{9,14},{10,... | collective-permute-start | bytes 196616 | tf_op jit(solution)/shard_map/ppermute | solution.py:281
  27.0 8.5 %collective-permute-start.7 = (f32[2,1024]{1,0:T(2,128)S(1)}, f32[2,1024]{1,0:T(2,128)S(1)}, u32[]{:S(2)}, u32[]{:S(2)}) collective-permute-start(f32[2,1024]{1,0:T(2,128)S(1)} %pad_maximum_fusion), channel_id=1, source_target_pairs={{0,96},{1,97},{2,98},{3,99},{4,100},{5,101},{6,102},{7,103},{8,64}... | collective-permute-start | bytes 24584 | tf_op jit(solution)/shard_map/ppermute | solution.py:272
  42.4 27.3 %all-to-all-start.1 = ((bf16[16,8,4,512]{3,2,1,0:T(4,128)(2,1)}), bf16[16,8,4,512]{3,2,1,0:T(4,128)(2,1)S(1)}, u32[]{:S(2)}, u32[]{:S(2)}) async-start(bf16[16,8,4,512]{3,2,1,0:T(4,128)(2,1)} %shard_map.65), calls=%async_computation.1 | async-start | bytes 1048576 | tf_op jit(solution)/shard_map/all_to_all | solution.py:287
  49.2 15.7 %copy-start = (f32[4]{0:T(128)S(1)}, f32[4]{0:T(128)}, u32[]{:S(2)}) copy-start(f32[4]{0:T(128)} %weight_ref.1) | copy-start | bytes 52
  49.2 6.8 %collective-permute-start.11 = (bf16[528,256]{1,0:T(8,128)(2,1)S(1)}, bf16[528,256]{1,0:T(8,128)(2,1)S(1)}, u32[]{:S(2)}, u32[]{:S(2)}) collective-permute-start(bf16[528,256]{1,0:T(8,128)(2,1)S(1)} %get-tuple-element.29), channel_id=1, source_target_pairs={{96,97},{97,96},{98,99},{99,98},{100,101},{101,100},{102,103},{103... | collective-permute-start | bytes 811016 | tf_op jit(solution)/shard_map/ppermute | solution.py:302
  50.9 8.1 %collective-permute-start.10 = (bf16[528,256]{1,0:T(8,128)(2,1)S(1)}, bf16[528,256]{1,0:T(8,128)(2,1)S(1)}, u32[]{:S(2)}, u32[]{:S(2)}) collective-permute-start(bf16[528,256]{1,0:T(8,128)(2,1)S(1)} %get-tuple-element.29), channel_id=1, source_target_pairs={{97,98},{98,97},{99,100},{100,99},{101,102},{102,101},{65,66},{66,... | collective-permute-start | bytes 811016 | tf_op jit(solution)/shard_map/ppermute | solution.py:302
  52.8 12.1 %collective-permute-start.9 = (bf16[528,256]{1,0:T(8,128)(2,1)S(1)}, bf16[528,256]{1,0:T(8,128)(2,1)S(1)}, u32[]{:S(2)}, u32[]{:S(2)}) collective-permute-start(bf16[528,256]{1,0:T(8,128)(2,1)S(1)} %get-tuple-element.29), channel_id=1, source_target_pairs={{64,32},{32,64},{65,33},{33,65},{66,34},{34,66},{67,35},{35,67},{6... | collective-permute-start | bytes 811016 | tf_op jit(solution)/shard_map/ppermute | solution.py:302
  55.9 9.0 %collective-permute-start.8 = (bf16[528,256]{1,0:T(8,128)(2,1)S(1)}, bf16[528,256]{1,0:T(8,128)(2,1)S(1)}, u32[]{:S(2)}, u32[]{:S(2)}) collective-permute-start(bf16[528,256]{1,0:T(8,128)(2,1)S(1)} %get-tuple-element.29), channel_id=1, source_target_pairs={{96,64},{64,96},{97,65},{65,97},{98,66},{66,98},{99,67},{67,99},{1... | collective-permute-start | bytes 811016 | tf_op jit(solution)/shard_map/ppermute | solution.py:302
where the time goes:
time: 97.7 us; the launch traced here: 97.3 us
  starting transfers between devices  39.6 us (41%)
  blocking collectives  26 us (27%)
  waiting for transfers between devices  21.5 us (22%)
  Pallas kernels  9.08 us (9%)
    all_to_all x1, blocking collectives, shards(): lax.all_to_all(analysis.reshape(128, 4, CELLS), 'mem', split_axis=0, conc...  26 us
    all_to_all x1, starting transfers between devices, shards(): lax.all_to_all(obs_ens.reshape(4, 128, LOCAL_OBS), 'mem', split_axis=1, c...  14.6 us
    ppermute x7, starting transfers between devices, shards(): parts[d] = lax.ppermute(parts[d], 'mem', [(k, k ^ d) for k in range(128)])  10 us
    ppermute x4, waiting for transfers between devices, shards(): received.append(lax.ppermute(send, ('grp', 'mem'), swaps(by, parity)))  8.84 us
    all_to_all x1, waiting for transfers between devices, shards(): lax.all_to_all(obs_ens.reshape(4, 128, LOCAL_OBS), 'mem', split_axis=1, c...  6.94 us
    ppermute x4, starting transfers between devices, shards(): received.append(lax.ppermute(send, ('grp', 'mem'), swaps(by, parity)))  6.8 us
    ppermute x7, waiting for transfers between devices, shards(): parts[d] = lax.ppermute(parts[d], 'mem', [(k, k ^ d) for k in range(128)])  5.71 us
    all_to_all x1, starting transfers between devices, shards(): lax.all_to_all(state, 'mem', split_axis=0, concat_axis=0, tiled=False, ax...  5.3 us
  transfers between devices with their start and end apart: 14, of which 7 were waited for; matrix products, arithmetic and copies ran while one was open for 0% of the time, Pallas kernels for 9%

commit v1 on v0

--- a/solution.py
+++ b/solution.py
@@ -100,7 +100,7 @@
         rows_ref[pl.ds(pl.multiple_of(i * 32, 32), 32)] = block.reshape(32, width).astype(BF16)
         return acc + jnp.sum(block, axis=0)
 
-    acc = lax.fori_loop(0, 16, step, jnp.zeros((8, width), F32))
+    acc = lax.fori_loop(0, 16, step, jnp.zeros((8, width), F32), unroll=4)
     return jnp.sum(acc, axis=0, keepdims=True) / MEMBERS
 
 
@@ -116,7 +116,7 @@
         left_ref[at] = (spread.astype(F32) * rates).astype(BF16)
         return carry
 
-    lax.fori_loop(0, 16, step, 0)
+    lax.fori_loop(0, 16, step, 0, unroll=4)
     innovation = (rates * (observed - centre)).astype(BF16)
     left_ref[pl.ds(MEMBERS, VEC)] = jnp.broadcast_to(innovation, (VEC, innovation.shape[1]))
     contract = (((1,), (1,)), ((), ()))
@@ -230,7 +230,7 @@
         dev_ref[pl.ds(pl.multiple_of(i * 32, 32), 32)] = block.astype(BF16)
         return acc + jnp.sum(block.reshape(4, 8, CELLS), axis=0)
 
-    acc = lax.fori_loop(0, 16, gather, jnp.zeros((8, CELLS), F32))
+    acc = lax.fori_loop(0, 16, gather, jnp.zeros((8, CELLS), F32), unroll=4)
     centre = jnp.sum(acc, axis=0, keepdims=True) / MEMBERS
     dev_ref[...] = (dev_ref[...].astype(F32) - centre).astype(BF16)
     update = jnp.dot(transform_ref[...], dev_ref[...], preferred_element_type=F32)

time: 97.7 us -> 97.6 us (level)
  no operation moved by 1% of the time
where the time goes in v1:
time: 97.6 us; the launch traced here: 97.2 us
  starting transfers between devices  39.6 us (41%)
  blocking collectives  26.1 us (27%)
  waiting for transfers between devices  21.5 us (22%)
  Pallas kernels  8.94 us (9%)
    all_to_all x1, blocking collectives, shards(): lax.all_to_all(analysis.reshape(128, 4, CELLS), 'mem', split_axis=0, conc...  26.1 us
    all_to_all x1, starting transfers between devices, shards(): lax.all_to_all(obs_ens.reshape(4, 128, LOCAL_OBS), 'mem', split_axis=1, c...  14.6 us
    ppermute x7, starting transfers between devices, shards(): parts[d] = lax.ppermute(parts[d], 'mem', [(k, k ^ d) for k in range(128)])  10 us
    ppermute x4, waiting for transfers between devices, shards(): received.append(lax.ppermute(send, ('grp', 'mem'), swaps(by, parity)))  8.81 us
    all_to_all x1, waiting for transfers between devices, shards(): lax.all_to_all(obs_ens.reshape(4, 128, LOCAL_OBS), 'mem', split_axis=1, c...  6.94 us
    ppermute x4, starting transfers between devices, shards(): received.append(lax.ppermute(send, ('grp', 'mem'), swaps(by, parity)))  6.8 us
    ppermute x7, waiting for transfers between devices, shards(): parts[d] = lax.ppermute(parts[d], 'mem', [(k, k ^ d) for k in range(128)])  5.71 us
    all_to_all x1, starting transfers between devices, shards(): lax.all_to_all(state, 'mem', split_axis=0, concat_axis=0, tiled=False, ax...  5.3 us
  transfers between devices with their start and end apart: 14, of which 7 were waited for; matrix products, arithmetic and copies ran while one was open for 0% of the time, Pallas kernels for 9%

profile of v1, /device:TPU:1, one launch (start us, length us, event | category | flops | bytes accessed | tf_op | source)
XLA Modules:
  0.0 97.2 jit_solution(15199293368316865180)
XLA Ops:
  0.0 14.6 %all-to-all-start = ((bf16[1,4,128,1024]{3,1,0,2:T(4,128)(2,1)}), bf16[1,4,128,1024]{3,1,0,2:T(4,128)(2,1)S(1)}, u32[]{:S(2)}, u32[]{:S(2)}) async-start(bf16[1,4,128,1024]{3,1,0,2:T(4,128)(2,1)} %bitcast.22), calls=%async_computation | async-start | bytes 2097152 | tf_op jit(solution)/shard_map/all_to_all | solution.py:267
  14.6 1.1 %shard_map.64 = (bf16[16,4,512]{2,1,0:T(4,128)(2,1)S(1)}, bf16[16,4,512]{2,1,0:T(4,128)(2,1)S(1)}, bf16[16,4,512]{2,1,0:T(4,128)(2,1)S(1)}, bf16[16,4,512]{2,1,0...) custom-call(bf16[16,8,4,512]{3,2,1,0:T(4,128)(2,1)} %bitcast.23), custom_call_target="tpu_custom_call" | custom-call | tf_op jit(solution)/shard_map/pallas_call | solution.py:276
  15.8 0.5 collective-permute-start
  16.3 0.0 copy-start.1
  16.3 1.2 %collective-permute-start.1 = (bf16[16,4,512]{2,1,0:T(4,128)(2,1)S(1)}, bf16[16,4,512]{2,1,0:T(4,128)(2,1)S(1)}, u32[]{:S(2)}, u32[]{:S(2)}) collective-permute-start(bf16[16,4,512]{2,1,0:T(4,128)(2,1)S(1)} %get-tuple-element.20), channel_id=1, source_target_pairs={{0,2},{1,3},{2,0},{3,1},{4,6},{5,7},{6,4},{7,5},{8,10},{9,11},{10,... | collective-permute-start | bytes 196616 | tf_op jit(solution)/shard_map/ppermute | solution.py:281
  17.5 0.6 collective-permute-start.2
  18.0 0.0 copy-start.3
  18.0 2.7 %collective-permute-start.3 = (bf16[16,4,512]{2,1,0:T(4,128)(2,1)S(1)}, bf16[16,4,512]{2,1,0:T(4,128)(2,1)S(1)}, u32[]{:S(2)}, u32[]{:S(2)}) collective-permute-start(bf16[16,4,512]{2,1,0:T(4,128)(2,1)S(1)} %get-tuple-element.22), channel_id=1, source_target_pairs={{0,4},{1,5},{2,6},{3,7},{4,0},{5,1},{6,2},{7,3},{8,12},{9,13},{10,... | collective-permute-start | bytes 196616 | tf_op jit(solution)/shard_map/ppermute | solution.py:281
  20.7 0.5 collective-permute-start.4
  21.3 0.0 copy-done.3
  21.3 0.0 copy-done.1
  21.3 0.1 select_reduce_fusion
  21.4 0.0 copy-start.2
  21.4 0.0 collective-permute-done.refs_1_
  21.4 2.5 %collective-permute-start.5 = (bf16[16,4,512]{2,1,0:T(4,128)(2,1)S(1)}, bf16[16,4,512]{2,1,0:T(4,128)(2,1)S(1)}, u32[]{:S(2)}, u32[]{:S(2)}) collective-permute-start(bf16[16,4,512]{2,1,0:T(4,128)(2,1)S(1)} %get-tuple-element.24), channel_id=1, source_target_pairs={{0,6},{1,7},{2,4},{3,5},{4,2},{5,3},{6,0},{7,1},{8,14},{9,15},{10,... | collective-permute-start | bytes 196616 | tf_op jit(solution)/shard_map/ppermute | solution.py:281
  23.9 0.0 collective-permute-done.1.refs_2_
  23.9 2.0 %collective-permute-start.6 = (bf16[16,4,512]{2,1,0:T(4,128)(2,1)S(1)}, bf16[16,4,512]{2,1,0:T(4,128)(2,1)S(1)}, u32[]{:S(2)}, u32[]{:S(2)}) collective-permute-start(bf16[16,4,512]{2,1,0:T(4,128)(2,1)S(1)} %get-tuple-element.25), channel_id=1, source_target_pairs={{0,7},{1,6},{2,5},{3,4},{4,3},{5,2},{6,1},{7,0},{8,15},{9,14},{10,... | collective-permute-start | bytes 196616 | tf_op jit(solution)/shard_map/ppermute | solution.py:281
  25.9 0.0 copy-done.2
  26.0 1.0 %collective-permute-done.2.refs_3_ = bf16[16,4,512]{2,1,0:T(4,128)(2,1)S(1)} collective-permute-done((bf16[16,4,512]{2,1,0:T(4,128)(2,1)S(1)}, bf16[16,4,512]{2,1,0:T(4,128)(2,1)S(1)}, u32[]{:S(2)}, u32[]{:S(2)}) %collective-permute-start.2) | collective-permute-done | bytes 65568 | tf_op jit(solution)/shard_map/ppermute | solution.py:281
  27.0 2.9 %collective-permute-start.7 = (f32[2,1024]{1,0:T(2,128)S(1)}, f32[2,1024]{1,0:T(2,128)S(1)}, u32[]{:S(2)}, u32[]{:S(2)}) collective-permute-start(f32[2,1024]{1,0:T(2,128)S(1)} %pad_maximum_fusion), channel_id=1, source_target_pairs={{0,96},{1,97},{2,98},{3,99},{4,100},{5,101},{6,102},{7,103},{8,64}... | collective-permute-start | bytes 24584 | tf_op jit(solution)/shard_map/ppermute | solution.py:272
  29.9 0.3 collective-permute-done.3.refs_4_
  30.2 2.0 %collective-permute-done.4.refs_5_ = bf16[16,4,512]{2,1,0:T(4,128)(2,1)S(1)} collective-permute-done((bf16[16,4,512]{2,1,0:T(4,128)(2,1)S(1)}, bf16[16,4,512]{2,1,0:T(4,128)(2,1)S(1)}, u32[]{:S(2)}, u32[]{:S(2)}) %collective-permute-start.4) | collective-permute-done | bytes 65568 | tf_op jit(solution)/shard_map/ppermute | solution.py:281
  32.2 0.0 collective-permute-done.5.refs_6_
  32.2 2.4 %collective-permute-done.6.refs_7_ = bf16[16,4,512]{2,1,0:T(4,128)(2,1)S(1)} collective-permute-done((bf16[16,4,512]{2,1,0:T(4,128)(2,1)S(1)}, bf16[16,4,512]{2,1,0:T(4,128)(2,1)S(1)}, u32[]{:S(2)}, u32[]{:S(2)}) %collective-permute-start.6) | collective-permute-done | bytes 65568 | tf_op jit(solution)/shard_map/ppermute | solution.py:281
  34.6 0.8 shard_map.65
  35.4 0.0 collective-permute-done.7.val_ref
  35.4 6.9 %all-to-all-done = bf16[1,4,128,1024]{3,1,0,2:T(4,128)(2,1)S(1)} async-done(((bf16[1,4,128,1024]{3,1,0,2:T(4,128)(2,1)}), bf16[1,4,128,1024]{3,1,0,2:T(4,128)(2,1)S(1)}, u32[]{:S(2)}, u32[]{:S(2)}) %all-to-all-start) | async-done | bytes 1048608 | tf_op jit(solution)/shard_map/all_to_all | solution.py:267
  42.4 5.3 %all-to-all-start.1 = ((bf16[16,8,4,512]{3,2,1,0:T(4,128)(2,1)}), bf16[16,8,4,512]{3,2,1,0:T(4,128)(2,1)S(1)}, u32[]{:S(2)}, u32[]{:S(2)}) async-start(bf16[16,8,4,512]{3,2,1,0:T(4,128)(2,1)} %shard_map.65), calls=%async_computation.1 | async-start | bytes 1048576 | tf_op jit(solution)/shard_map/all_to_all | solution.py:287
  47.7 1.5 %shard_map.66 = (f32[528,256]{1,0:T(8,128)S(1)}, bf16[528,256]{1,0:T(8,128)(2,1)S(1)}) custom-call(bf16[64,2,4,1024]{3,2,1,0:T(4,128)(2,1)S(1)} %bitcast.19, f32[2,1024]{1,0:T(2,128)S(1)} %collective-permute-done.7.val_ref), custom_call_target="tpu_custom_call" | custom-call | tf_op jit(solution)/shard_map/pallas_call | solution.py:293
  49.2 0.0 copy-start
  49.2 1.7 %collective-permute-start.11 = (bf16[528,256]{1,0:T(8,128)(2,1)S(1)}, bf16[528,256]{1,0:T(8,128)(2,1)S(1)}, u32[]{:S(2)}, u32[]{:S(2)}) collective-permute-start(bf16[528,256]{1,0:T(8,128)(2,1)S(1)} %get-tuple-element.29), channel_id=1, source_target_pairs={{96,97},{97,96},{98,99},{99,98},{100,101},{101,100},{102,103},{103... | collective-permute-start | bytes 811016 | tf_op jit(solution)/shard_map/ppermute | solution.py:302
  50.9 1.9 %collective-permute-start.10 = (bf16[528,256]{1,0:T(8,128)(2,1)S(1)}, bf16[528,256]{1,0:T(8,128)(2,1)S(1)}, u32[]{:S(2)}, u32[]{:S(2)}) collective-permute-start(bf16[528,256]{1,0:T(8,128)(2,1)S(1)} %get-tuple-element.29), channel_id=1, source_target_pairs={{97,98},{98,97},{99,100},{100,99},{101,102},{102,101},{65,66},{66,... | collective-permute-start | bytes 811016 | tf_op jit(solution)/shard_map/ppermute | solution.py:302
  52.8 3.1 %collective-permute-start.9 = (bf16[528,256]{1,0:T(8,128)(2,1)S(1)}, bf16[528,256]{1,0:T(8,128)(2,1)S(1)}, u32[]{:S(2)}, u32[]{:S(2)}) collective-permute-start(bf16[528,256]{1,0:T(8,128)(2,1)S(1)} %get-tuple-element.29), channel_id=1, source_target_pairs={{64,32},{32,64},{65,33},{33,65},{66,34},{34,66},{67,35},{35,67},{6... | collective-permute-start | bytes 811016 | tf_op jit(solution)/shard_map/ppermute | solution.py:302
  55.9 0.1 collective-permute-start.8
  56.0 0.0 collective-permute-done.11.ew0_ref
  56.0 2.9 %collective-permute-done.10.ew1_ref = bf16[528,256]{1,0:T(8,128)(2,1)S(1)} collective-permute-done((bf16[528,256]{1,0:T(8,128)(2,1)S(1)}, bf16[528,256]{1,0:T(8,128)(2,1)S(1)}, u32[]{:S(2)}, u32[]{:S(2)}) %collective-permute-start.10) | collective-permute-done | bytes 270368 | tf_op jit(solution)/shard_map/ppermute | solution.py:302
  58.9 5.9 %collective-permute-done.9.ns1_ref = bf16[528,256]{1,0:T(8,128)(2,1)S(1)} collective-permute-done((bf16[528,256]{1,0:T(8,128)(2,1)S(1)}, bf16[528,256]{1,0:T(8,128)(2,1)S(1)}, u32[]{:S(2)}, u32[]{:S(2)}) %collective-permute-start.9) | collective-permute-done | bytes 270368 | tf_op jit(solution)/shard_map/ppermute | solution.py:302
  64.8 0.0 collective-permute-done.8.ns0_ref
  64.8 0.0 copy-done
  64.8 4.8 %shard_map.67.transform_ref = bf16[512,512]{1,0:T(8,128)(2,1)S(1)} custom-call(f32[4]{0:T(128)S(1)} %copy-done, f32[528,256]{1,0:T(8,128)S(1)} %get-tuple-element.28.own_ref, bf16[528,256]{1,0:T(8,128)(2,1)S(1)} %collective-permute-done.8.ns0_ref, bf16[528,256]{1,0:T(8,128)(2,1)S(1)} %collective-permute-done.9.ns1_ref, ...), custom_call_target="tpu_custom_call" | custom-call | tf_op jit(solution)/shard_map/pallas_call | solution.py:304
  69.6 0.0 all-to-all-done.1.state_ref
  69.6 0.7 shard_map.68
  70.3 26.1 %all_to_all.35 = bf16[128,4,1,512]{3,1,2,0:T(4,128)(2,1)S(1)} all-to-all(bf16[128,4,1,512]{3,1,2,0:T(4,128)(2,1)S(1)} %bitcast.20), channel_id=1, replica_groups={{96,97,98,99,100,101,102,103,64,65,66,67,68,69,70,71,32,33,34,35,36,37,..., dimensions={0} | all-to-all | bytes 1048576 | tf_op jit(solution)/shard_map/all_to_all | solution.py:312
  96.4 0.8 copy.12
  (2 shorter events, 0.0 us)
Async XLA Ops:
  0.0 42.4 %all-to-all-start = ((bf16[1,4,128,1024]{3,1,0,2:T(4,128)(2,1)}), bf16[1,4,128,1024]{3,1,0,2:T(4,128)(2,1)S(1)}, u32[]{:S(2)}, u32[]{:S(2)}) async-start(bf16[1,4,128,1024]{3,1,0,2:T(4,128)(2,1)} %bitcast.22), calls=%async_computation | async-start | bytes 2097152 | tf_op jit(solution)/shard_map/all_to_all | solution.py:267
  15.8 5.6 %collective-permute-start = (bf16[16,4,512]{2,1,0:T(4,128)(2,1)S(1)}, bf16[16,4,512]{2,1,0:T(4,128)(2,1)S(1)}, u32[]{:S(2)}, u32[]{:S(2)}) collective-permute-start(bf16[16,4,512]{2,1,0:T(4,128)(2,1)S(1)} %get-tuple-element.19), channel_id=1, source_target_pairs={{0,1},{1,0},{2,3},{3,2},{4,5},{5,4},{6,7},{7,6},{8,9},{9,8},{10,11... | collective-permute-start | bytes 196616 | tf_op jit(solution)/shard_map/ppermute | solution.py:281
  16.3 5.0 %copy-start.1 = (s32[1024]{0:T(1024)S(1)}, s32[1024]{0:T(1024)}, u32[]{:S(2)}) copy-start(s32[1024]{0:T(1024)} %param.9) | copy-start | bytes 12292
  16.3 7.6 %collective-permute-start.1 = (bf16[16,4,512]{2,1,0:T(4,128)(2,1)S(1)}, bf16[16,4,512]{2,1,0:T(4,128)(2,1)S(1)}, u32[]{:S(2)}, u32[]{:S(2)}) collective-permute-start(bf16[16,4,512]{2,1,0:T(4,128)(2,1)S(1)} %get-tuple-element.20), channel_id=1, source_target_pairs={{0,2},{1,3},{2,0},{3,1},{4,6},{5,7},{6,4},{7,5},{8,10},{9,11},{10,... | collective-permute-start | bytes 196616 | tf_op jit(solution)/shard_map/ppermute | solution.py:281
  17.5 9.5 %collective-permute-start.2 = (bf16[16,4,512]{2,1,0:T(4,128)(2,1)S(1)}, bf16[16,4,512]{2,1,0:T(4,128)(2,1)S(1)}, u32[]{:S(2)}, u32[]{:S(2)}) collective-permute-start(bf16[16,4,512]{2,1,0:T(4,128)(2,1)S(1)} %get-tuple-element.21), channel_id=1, source_target_pairs={{0,3},{1,2},{2,1},{3,0},{4,7},{5,6},{6,5},{7,4},{8,11},{9,10},{10,... | collective-permute-start | bytes 196616 | tf_op jit(solution)/shard_map/ppermute | solution.py:281
  18.0 3.2 %copy-start.3 = (bf16[16]{0:T(256)(128)(2,1)S(1)}, bf16[16]{0:T(256)(128)(2,1)}, u32[]{:S(2)}) copy-start(bf16[16]{0:T(256)(128)(2,1)} %param.10) | copy-start | bytes 100
  18.0 12.1 %collective-permute-start.3 = (bf16[16,4,512]{2,1,0:T(4,128)(2,1)S(1)}, bf16[16,4,512]{2,1,0:T(4,128)(2,1)S(1)}, u32[]{:S(2)}, u32[]{:S(2)}) collective-permute-start(bf16[16,4,512]{2,1,0:T(4,128)(2,1)S(1)} %get-tuple-element.22), channel_id=1, source_target_pairs={{0,4},{1,5},{2,6},{3,7},{4,0},{5,1},{6,2},{7,3},{8,12},{9,13},{10,... | collective-permute-start | bytes 196616 | tf_op jit(solution)/shard_map/ppermute | solution.py:281
  20.7 11.4 %collective-permute-start.4 = (bf16[16,4,512]{2,1,0:T(4,128)(2,1)S(1)}, bf16[16,4,512]{2,1,0:T(4,128)(2,1)S(1)}, u32[]{:S(2)}, u32[]{:S(2)}) collective-permute-start(bf16[16,4,512]{2,1,0:T(4,128)(2,1)S(1)} %get-tuple-element.23), channel_id=1, source_target_pairs={{0,5},{1,4},{2,7},{3,6},{4,1},{5,0},{6,3},{7,2},{8,13},{9,12},{10,... | collective-permute-start | bytes 196616 | tf_op jit(solution)/shard_map/ppermute | solution.py:281
  21.4 4.6 %copy-start.2 = (f32[1024]{0:T(1024)S(1)}, f32[1024]{0:T(1024)}, u32[]{:S(2)}) copy-start(f32[1024]{0:T(1024)} %param.8) | copy-start | bytes 12292
  21.4 10.8 %collective-permute-start.5 = (bf16[16,4,512]{2,1,0:T(4,128)(2,1)S(1)}, bf16[16,4,512]{2,1,0:T(4,128)(2,1)S(1)}, u32[]{:S(2)}, u32[]{:S(2)}) collective-permute-start(bf16[16,4,512]{2,1,0:T(4,128)(2,1)S(1)} %get-tuple-element.24), channel_id=1, source_target_pairs={{0,6},{1,7},{2,4},{3,5},{4,2},{5,3},{6,0},{7,1},{8,14},{9,15},{10,... | collective-permute-start | bytes 196616 | tf_op jit(solution)/shard_map/ppermute | solution.py:281
  23.9 10.7 %collective-permute-start.6 = (bf16[16,4,512]{2,1,0:T(4,128)(2,1)S(1)}, bf16[16,4,512]{2,1,0:T(4,128)(2,1)S(1)}, u32[]{:S(2)}, u32[]{:S(2)}) collective-permute-start(bf16[16,4,512]{2,1,0:T(4,128)(2,1)S(1)} %get-tuple-element.25), channel_id=1, source_target_pairs={{0,7},{1,6},{2,5},{3,4},{4,3},{5,2},{6,1},{7,0},{8,15},{9,14},{10,... | collective-permute-start | bytes 196616 | tf_op jit(solution)/shard_map/ppermute | solution.py:281
  27.0 8.5 %collective-permute-start.7 = (f32[2,1024]{1,0:T(2,128)S(1)}, f32[2,1024]{1,0:T(2,128)S(1)}, u32[]{:S(2)}, u32[]{:S(2)}) collective-permute-start(f32[2,1024]{1,0:T(2,128)S(1)} %pad_maximum_fusion), channel_id=1, source_target_pairs={{0,96},{1,97},{2,98},{3,99},{4,100},{5,101},{6,102},{7,103},{8,64}... | collective-permute-start | bytes 24584 | tf_op jit(solution)/shard_map/ppermute | solution.py:272
  42.4 27.2 %all-to-all-start.1 = ((bf16[16,8,4,512]{3,2,1,0:T(4,128)(2,1)}), bf16[16,8,4,512]{3,2,1,0:T(4,128)(2,1)S(1)}, u32[]{:S(2)}, u32[]{:S(2)}) async-start(bf16[16,8,4,512]{3,2,1,0:T(4,128)(2,1)} %shard_map.65), calls=%async_computation.1 | async-start | bytes 1048576 | tf_op jit(solution)/shard_map/all_to_all | solution.py:287
  49.2 15.7 %copy-start = (f32[4]{0:T(128)S(1)}, f32[4]{0:T(128)}, u32[]{:S(2)}) copy-start(f32[4]{0:T(128)} %weight_ref.1) | copy-start | bytes 52
  49.2 6.8 %collective-permute-start.11 = (bf16[528,256]{1,0:T(8,128)(2,1)S(1)}, bf16[528,256]{1,0:T(8,128)(2,1)S(1)}, u32[]{:S(2)}, u32[]{:S(2)}) collective-permute-start(bf16[528,256]{1,0:T(8,128)(2,1)S(1)} %get-tuple-element.29), channel_id=1, source_target_pairs={{96,97},{97,96},{98,99},{99,98},{100,101},{101,100},{102,103},{103... | collective-permute-start | bytes 811016 | tf_op jit(solution)/shard_map/ppermute | solution.py:302
  50.9 8.1 %collective-permute-start.10 = (bf16[528,256]{1,0:T(8,128)(2,1)S(1)}, bf16[528,256]{1,0:T(8,128)(2,1)S(1)}, u32[]{:S(2)}, u32[]{:S(2)}) collective-permute-start(bf16[528,256]{1,0:T(8,128)(2,1)S(1)} %get-tuple-element.29), channel_id=1, source_target_pairs={{97,98},{98,97},{99,100},{100,99},{101,102},{102,101},{65,66},{66,... | collective-permute-start | bytes 811016 | tf_op jit(solution)/shard_map/ppermute | solution.py:302
  52.8 12.0 %collective-permute-start.9 = (bf16[528,256]{1,0:T(8,128)(2,1)S(1)}, bf16[528,256]{1,0:T(8,128)(2,1)S(1)}, u32[]{:S(2)}, u32[]{:S(2)}) collective-permute-start(bf16[528,256]{1,0:T(8,128)(2,1)S(1)} %get-tuple-element.29), channel_id=1, source_target_pairs={{64,32},{32,64},{65,33},{33,65},{66,34},{34,66},{67,35},{35,67},{6... | collective-permute-start | bytes 811016 | tf_op jit(solution)/shard_map/ppermute | solution.py:302
  55.9 8.9 %collective-permute-start.8 = (bf16[528,256]{1,0:T(8,128)(2,1)S(1)}, bf16[528,256]{1,0:T(8,128)(2,1)S(1)}, u32[]{:S(2)}, u32[]{:S(2)}) collective-permute-start(bf16[528,256]{1,0:T(8,128)(2,1)S(1)} %get-tuple-element.29), channel_id=1, source_target_pairs={{96,64},{64,96},{97,65},{65,97},{98,66},{66,98},{99,67},{67,99},{1... | collective-permute-start | bytes 811016 | tf_op jit(solution)/shard_map/ppermute | solution.py:302
